TPU v7x, 32 devices: a whole 2x2x4 slice. The times are simulated.
32 devices in a mesh: radial: 8 (over y, x, core), mode: 4 (over z).
Axes of the slice: x: 2, y: 2, z: 4, core: 2. Of those that a mesh axis runs over, the one named last changes fastest.
Arguments:
- scalar_field: float32 [256, 64, 2, 384], P('radial', 'mode'), may hold values from -48 to 48
- radial_flow: float32 [256, 64, 2, 384], P('radial', 'mode'), may hold values from -6 to 6
- legendre: bfloat16 [64, 384, 768], P('mode'), may hold values from -0.3125 to 0.3125
- diffusivity: float32 [256], P('radial'), may hold values from 1000 to 100000
Outputs:
- field_new: float32 [256, 64, 2, 384], P('radial', 'mode')
All inputs are finite; a program needn't handle non-finite values.
Results may differ from a plain program's by a relative error of at most 0.0071.
Values may be sent and summed in bfloat16 or wider, within the bound.
A program may use at most 128 MiB of HBM per device.

v0:
```python
import math
import jax
import jax.numpy as jnp
from jax import lax
from jax.sharding import PartitionSpec as P

NLON = 1536


def prefix_2(value, axis, join, neutral, backward):
    count, mine = (lax.axis_size(axis), lax.axis_index(axis))
    pieces = jax.tree.map(lambda part: lax.all_gather(part, axis), value)
    if backward:
        pieces = jax.tree.map(lambda part: part[::-1], pieces)
        mine = count - 1 - mine
    total = jax.tree.map(
        lambda part, zero: jnp.full_like(part, 0) + jnp.asarray(zero, part.dtype), value, neutral
    )

    def hop(position, total):
        longer = join(total, jax.tree.map(lambda part: part[position], pieces))
        return jax.tree.map(lambda new, old: jnp.where(position < mine, new, old), longer, total)

    return lax.fori_loop(0, count - 1, hop, total)


def longitude_tables(orders, points):
    order_ids = jnp.arange(orders, dtype=jnp.int32)
    point_ids = jnp.arange(points, dtype=jnp.int32)
    phase = order_ids[:, None] * point_ids[None, :] % points
    angle = phase.astype(jnp.float32) * (2.0 * math.pi / points)
    cosine = jnp.cos(angle)
    sine_part = jnp.sin(angle)
    paired = jnp.stack([cosine, -sine_part], axis=1)
    synth_table = (paired / math.sqrt(orders)).astype(jnp.bfloat16)
    analysis_table = (paired * math.sqrt(2.0 / points)).astype(jnp.bfloat16)
    return (synth_table, analysis_table)


def normalized(matrix):
    largest = jnp.max(jnp.abs(matrix), axis=(0, 1))
    return matrix / largest


def combine_maps(earlier, later):
    return normalized(jnp.sum(later[:, :, None] * earlier[None, :, :], axis=1))


def combine_affine(earlier, later):
    return (later[0] + later[1][:, None, :] * earlier[0], later[1] * earlier[1])


def on_device(scalar_field, radial_flow, legendre, diffusivity):
    shells, ord_dev, halves, degrees = scalar_field.shape
    orders = ord_dev * lax.axis_size("mode")
    synth_table, analysis_table = longitude_tables(orders, NLON)
    field_lat = jnp.einsum(
        "rmcj,mjt->rmct",
        scalar_field.astype(jnp.bfloat16),
        legendre,
        preferred_element_type=jnp.float32,
    ).astype(jnp.bfloat16)
    flow_lat = jnp.einsum(
        "rmcj,mjt->rmct",
        radial_flow.astype(jnp.bfloat16),
        legendre,
        preferred_element_type=jnp.float32,
    ).astype(jnp.bfloat16)
    field_piece = lax.all_to_all(field_lat, "mode", split_axis=3, concat_axis=1, tiled=True)
    flow_piece = lax.all_to_all(flow_lat, "mode", split_axis=3, concat_axis=1, tiled=True)
    field_grid = jnp.einsum(
        "rmct,mcp->rtp", field_piece, synth_table, preferred_element_type=jnp.float32
    )
    flow_grid = jnp.einsum(
        "rmct,mcp->rtp", flow_piece, synth_table, preferred_element_type=jnp.float32
    )
    product = (field_grid * flow_grid).astype(jnp.bfloat16)
    modes_grid = jnp.einsum(
        "rtp,mcp->rmct", product, analysis_table, preferred_element_type=jnp.float32
    ).astype(jnp.bfloat16)
    spectral_back = lax.all_to_all(modes_grid, "mode", split_axis=1, concat_axis=3, tiled=True)
    forcing = jnp.einsum(
        "rmct,mjt->rmcj", spectral_back, legendre, preferred_element_type=jnp.float32
    )
    right_side = scalar_field + forcing
    radial_index = lax.axis_index("radial")
    nr_total = shells * lax.axis_size("radial")
    offset = nr_total * 7 // 13
    order_ids = (jnp.arange(ord_dev, dtype=jnp.int32) + lax.axis_index("mode") * ord_dev).astype(
        jnp.float32
    )
    degree = order_ids[:, None] + jnp.arange(degrees, dtype=jnp.float32)[None, :]
    angular = degree * (degree + 1.0)
    global_shells = radial_index * shells + jnp.arange(shells, dtype=jnp.int32)

    def coefficients(kappa_shell, shell_index):
        lower = jnp.where(shell_index > 0, -kappa_shell, 0.0)
        upper = jnp.where(shell_index < nr_total - 1, -kappa_shell, 0.0)
        radius = (offset + shell_index).astype(jnp.float32)
        diagonal = 1.0 + 2.0 * kappa_shell + kappa_shell * angular / (radius * radius)
        return (lower, upper, diagonal)

    identity = jnp.broadcast_to(
        jnp.eye(4, dtype=jnp.float32)[:, :, None, None], (4, 4, ord_dev, degrees)
    )

    def compose(composite, inputs):
        kappa_shell, source, shell_index = inputs
        lower, upper, diagonal = coefficients(kappa_shell, shell_index)
        new_rows = jnp.stack(
            [
                upper * composite[3],
                -lower * composite[1] + source[:, 0, :] * composite[3],
                -lower * composite[2] + source[:, 1, :] * composite[3],
                -lower * composite[0] + diagonal * composite[3],
            ]
        )
        return (normalized(new_rows), None)

    transfer, _ = lax.scan(compose, identity, (diffusivity, right_side, global_shells))
    prefix = prefix_2(transfer, "radial", combine_maps, identity, False)
    incoming = prefix[:, 3]
    ratio_start = incoming[0] / incoming[3]
    value_start = jnp.stack([incoming[1], incoming[2]], axis=1) / incoming[3][:, None, :]

    def sweep(carry, inputs):
        ratio_prev, value_prev = carry
        kappa_shell, source, shell_index = inputs
        lower, upper, diagonal = coefficients(kappa_shell, shell_index)
        pivot = diagonal - lower * ratio_prev
        ratio_now = upper / pivot
        value_now = (source - lower * value_prev) / pivot[:, None, :]
        return ((ratio_now, value_now), (ratio_now, value_now))

    _, (ratios, values) = lax.scan(
        sweep, (ratio_start, value_start), (diffusivity, right_side, global_shells)
    )

    def back_compose(carry, inputs):
        alpha, slope = carry
        ratio_now, value_now = inputs
        alpha = value_now - ratio_now[:, None, :] * alpha
        slope = -ratio_now * slope
        return ((alpha, slope), (alpha, slope))

    blank_value = jnp.zeros((ord_dev, halves, degrees), jnp.float32)
    unity = jnp.ones((ord_dev, degrees), jnp.float32)
    (alpha_dev, slope_dev), (alpha_all, slope_all) = lax.scan(
        back_compose, (blank_value, unity), (ratios, values), reverse=True
    )
    beyond, _ = prefix_2(
        (alpha_dev, slope_dev), "radial", combine_affine, (blank_value, unity), True
    )
    return alpha_all + slope_all[:, :, None, :] * beyond[None]


def solution(mesh):
    return jax.shard_map(
        on_device,
        mesh=mesh,
        in_specs=(
            P("radial", "mode", None, None),
            P("radial", "mode", None, None),
            P("mode", None, None),
            P("radial"),
        ),
        out_specs=P("radial", "mode", None, None),
        check_vma=False,
    )
```

profile of v0, /device:TPU:0, one launch (start us, length us, event | category | flops | bytes accessed | tf_op | source)
XLA Modules:
  0.0 700.0 jit_solution(18119201527040543334)
XLA Ops:
  8.5 5.2 fusion.40
  13.7 11.3 %copy.50 = bf16[32,16,2,768]{0,2,1,3:T(2,128)(2,1)} copy(bf16[32,16,2,768]{3,0,2,1:T(8,128)(2,1)S(1)} %fusion.40) | data formatting | bytes 3145728 | tf_op jit(solution)/shard_map/convert_element_type | solution.py:62
  25.0 8.3 %reshape.119 = bf16[4,2,98304]{2,1,0:T(2,128)(2,1)} reshape(bf16[768,16,2,32]{3,2,1,0:T(2,128)(2,1)} %bitcast.170) | data formatting | bytes 3145728
  33.3 6.5 all-to-all-start
  40.4 5.2 fusion.37
  45.6 11.3 %copy.54 = bf16[32,16,2,768]{0,2,1,3:T(2,128)(2,1)} copy(bf16[32,16,2,768]{3,0,2,1:T(8,128)(2,1)S(1)} %fusion.37) | data formatting | bytes 3145728 | tf_op jit(solution)/shard_map/convert_element_type | solution.py:68
  56.9 8.3 %reshape.121 = bf16[4,2,98304]{2,1,0:T(2,128)(2,1)} reshape(bf16[768,16,2,32]{3,2,1,0:T(2,128)(2,1)} %bitcast.171) | data formatting | bytes 3145728
  65.2 11.6 %all-to-all-done = bf16[4,2,98304]{2,1,0:T(2,128)(2,1)S(1)} async-done(((bf16[4,2,98304]{2,1,0:T(2,128)(2,1)}), bf16[4,2,98304]{2,1,0:T(2,128)(2,1)S(1)}, u32[]{:S(2)}, u32[]{:S(2)}) %all-to-all-start) | async-done | bytes 1572896 | tf_op jit(solution)/shard_map/all_to_all | solution.py:69
  76.8 4.5 all-to-all-start.1
  82.9 4.7 reshape.120
  87.6 20.9 %copy.68 = bf16[32,16,2,4,192]{4,3,1,2,0:T(4,128)(2,1)} copy(bf16[32,16,2,4,192]{0,2,1,4,3:T(2,128)(2,1)} %bitcast.172) | data formatting | bytes 3145728 | tf_op jit(solution)/shard_map/all_to_all | solution.py:69
  108.5 2.1 copy.52
  110.5 7.2 %all-to-all-done.1 = bf16[4,2,98304]{2,1,0:T(2,128)(2,1)} async-done(((bf16[4,2,98304]{2,1,0:T(2,128)(2,1)}), bf16[4,2,98304]{2,1,0:T(2,128)(2,1)}, u32[]{:S(2)}, u32[]{:S(2)}) %all-to-all-start.1) | async-done | bytes 1572896 | tf_op jit(solution)/shard_map/all_to_all | solution.py:70
  117.7 6.4 reshape.122
  124.1 20.9 %copy.69 = bf16[32,16,2,4,192]{4,3,1,2,0:T(4,128)(2,1)} copy(bf16[32,16,2,4,192]{0,2,1,4,3:T(2,128)(2,1)} %bitcast.173) | data formatting | bytes 3145728 | tf_op jit(solution)/shard_map/all_to_all | solution.py:70
  145.0 3.4 copy.56
  148.4 14.8 %fusion.52 = f32[32,192,1536,1]{2,1,3,0:T(8,128)} fusion(bf16[32,64,2,192]{3,1,2,0:T(8,128)(2,1)S(1)} %bitcast.174, f32[64,1,1536]{2,0,1:T(8,128)S(1)} %get-tuple-element.644, f32[64,1,1536]{2,0,1:T(8,128)S(1)} %get-tuple-element.645), kind=kOutput, calls=%fused_computation.71 | convolution fusion | flops 2416508928 | bytes 40108032 | tf_op jit(solution)/shard_map/rmct,mcp->rtp/dot_general | solution.py:71
  163.1 17.3 %convert_bitcast_fusion = bf16[32,64,2,192]{3,1,0,2:T(8,128)(2,1)S(1)} fusion(f32[32,192,1536,1]{2,1,3,0:T(8,128)} %fusion.52, bf16[32,64,2,192]{3,1,2,0:T(8,128)(2,1)} %bitcast.179, f32[64,1,1536]{2,0,1:T(8,128)S(1)} %get-tuple-element.644, f32[64,1,1536]{2,0,1:T(8,128)S(1)} %get-tuple-element.645), kind=kOutput, calls=%fused_computation.54 | convolution fusion | flops 4852678656 | bytes 41680896 | tf_op jit(solution)/shard_map/rtp,mcp->rmct/dot_general | solution.py:78
  180.5 2.5 copy.57
  183.0 3.6 all-to-all-start.2
  186.9 47.4 %all-to-all-done.2 = bf16[32,64,2,192]{3,0,2,1:T(8,128)(2,1)S(1)} async-done(((bf16[32,64,2,192]{3,0,2,1:T(8,128)(2,1)}), bf16[32,64,2,192]{3,0,2,1:T(8,128)(2,1)S(1)}, u32[]{:S(2)}, u32[]{:S(2)}) %all-to-all-start.2) | async-done | bytes 1572896 | tf_op jit(solution)/shard_map/all_to_all | solution.py:81
  235.7 3.6 copy.86
  239.2 2.8 all_to_all.50
  242.1 7.6 %bitcast_add_fusion.1 = f32[32,16,2,384]{3,0,2,1:T(8,128)S(1)} fusion(f32[32,16,2,384]{3,2,1,0:T(2,128)} %param.14, bf16[32,16,2,768]{3,0,2,1:T(8,128)(2,1)} %all_to_all.50, bf16[16,384,768]{2,1,0:T(8,128)(2,1)} %param.16), kind=kOutput, calls=%fused_computation.57 | convolution fusion | flops 604372992 | bytes 14155776 | tf_op jit(solution)/shard_map/rmct,mjt->rmcj/dot_general | solution.py:82
  249.8 164.0 %while.77 = (s32[]{:T(128)}, f32[4,4,16,384]{3,2,1,0:T(8,128)S(1)}, s32[32]{0:T(128)S(1)}, f32[32]{0:T(128)S(1)}, f32[32,16,2,384]{3,0,2,1:T(8,128)S(1)}, /*inde...) while((s32[]{:T(128)}, f32[4,4,16,384]{3,2,1,0:T(8,128)S(1)}, ...), condition=%wide.region_2.3_spmd.clone, body=%wide.region_0.2_spmd.clone.sunk | while | flops 1161229 | bytes 2408801 | solution.py:120
  414.5 31.4 %all-gather.5.cloned.1.call-done = f32[32,4,16,384]{3,2,1,0:T(8,128)} async-done(((f32[4,4,16,384]{3,2,1,0:T(8,128)}), f32[32,4,16,384]{3,2,1,0:T(8,128)}) %all-gather.5.cloned.1.call-update) | async-done | bytes 3145744 | tf_op jit(solution)/shard_map/all_gather | solution.py:12
  446.0 9.0 %while.76 = (s32[]{:T(128)}, f32[4,4,16,384]{3,2,1,0:T(8,128)S(1)}, s32[]{:T(128)}, f32[8,4,4,16,384]{4,3,2,1,0:T(8,128)}, s32[]{:T(128)}) while((s32[]{:T(128)}, f32[4,4,16,384]{3,2,1,0:T(8,128)S(1)}, s32[]{:T(128)}, f32[8,4,4,16,384]{4,3,2,1,0:T(8,128)}, s32[]{:T(128)}) %tuple.172), condition=%wide.region_6.7_spmd, body=%wide.region_3.6_spmd.sunk | while | flops 1075203 | bytes 3588171 | solution.py:24
  457.4 185.0 %while.78 = (s32[]{:T(128)}, f32[16,384]{1,0:T(8,128)S(1)}, f32[16,2,384]{2,1,0:T(2,128)S(1)}, f32[32,16,384]{2,1,0:T(8,128)S(1)}, f32[32,16,2,384]{3,2,1,0:T(2,...) while((s32[]{:T(128)}, f32[16,384]{1,0:T(8,128)S(1)}, ...), condition=%wide.region_8.9_spmd.clone, body=%wide.region_7.8_spmd.clone.sunk | while | flops 92172 | bytes 419129 | solution.py:135
  643.1 29.2 %while.79 = (s32[]{:T(128)}, f32[16,2,384]{2,1,0:T(2,128)S(1)}, f32[16,384]{1,0:T(8,128)S(1)}, f32[32,16,2,384]{3,2,1,0:T(2,128)S(1)}, f32[32,16,384]{2,1,0:T(8,...) while((s32[]{:T(128)}, f32[16,2,384]{2,1,0:T(2,128)S(1)}, ...), condition=%wide.region_10.11_spmd.clone, body=%wide.region_9.10_spmd.clone.sunk | while | flops 55300 | bytes 344196 | solution.py:148
  672.4 9.5 %all-gather.1 = f32[128,2,384]{2,1,0:T(2,128)S(1)} all-gather(f32[16,2,384]{2,1,0:T(2,128)S(1)} %get-tuple-element.408), channel_id=3, replica_groups=mesh['radial'=8,'mode'=4] {'radial'}, dimensions={0}, use_global_device_ids=true | all-gather | bytes 442368 | tf_op jit(solution)/shard_map/all_gather | solution.py:12
  682.0 8.3 %all-gather.2 = f32[128,384]{1,0:T(8,128)S(1)} all-gather(f32[16,384]{1,0:T(8,128)S(1)} %get-tuple-element.409), channel_id=4, replica_groups=mesh['radial'=8,'mode'=4] {'radial'}, dimensions={0}, use_global_device_ids=true | all-gather | bytes 221184 | tf_op jit(solution)/shard_map/all_gather | solution.py:12
  691.0 2.1 multiply_add_fusion.3
  (587 shorter events, 194.1 us)
Async XLA Ops:
  33.3 6.5 copy-start.2
  33.3 43.4 %all-to-all-start = ((bf16[4,2,98304]{2,1,0:T(2,128)(2,1)}), bf16[4,2,98304]{2,1,0:T(2,128)(2,1)S(1)}, u32[]{:S(2)}, u32[]{:S(2)}) async-start(bf16[4,2,98304]{2,1,0:T(2,128)(2,1)} %reshape.119), calls=%async_computation | async-start | bytes 3145728 | tf_op jit(solution)/shard_map/all_to_all | solution.py:69
  76.8 41.0 %all-to-all-start.1 = ((bf16[4,2,98304]{2,1,0:T(2,128)(2,1)}), bf16[4,2,98304]{2,1,0:T(2,128)(2,1)}, u32[]{:S(2)}, u32[]{:S(2)}) async-start(bf16[4,2,98304]{2,1,0:T(2,128)(2,1)} %reshape.121), calls=%async_computation.1 | async-start | bytes 3145728 | tf_op jit(solution)/shard_map/all_to_all | solution.py:70
  183.0 51.3 %all-to-all-start.2 = ((bf16[32,64,2,192]{3,0,2,1:T(8,128)(2,1)}), bf16[32,64,2,192]{3,0,2,1:T(8,128)(2,1)S(1)}, u32[]{:S(2)}, u32[]{:S(2)}) async-start(bf16[32,64,2,192]{3,0,2,1:T(8,128)(2,1)} %copy.57), calls=%async_computation.2 | async-start | bytes 4194304 | tf_op jit(solution)/shard_map/all_to_all | solution.py:81
  186.6 259.3 %all-gather.5.cloned.1.call-start = ((), (), s32[]{:S(2)}) async-start(), calls=%async_computation.3 | async-start | bytes 3538944 | tf_op jit(solution)/shard_map/all_gather | solution.py:12
  234.3 1.3 copy-start.1
  242.1 7.7 %copy-start.3 = (f32[32]{0:T(128)S(1)}, f32[32]{0:T(128)}, u32[]{:S(2)}) copy-start(f32[32]{0:T(128)} %param.17) | copy-start | bytes 388
  413.7 0.7 copy-start
Sparse Core Ops, SparseCore 0:
  414.6 31.2 all-gather.4
where the time goes:
time: 707 us; the launch traced here: 700 us
  loops' own time  204 us (29%)
  local copies, waits for them, and re-layouts  199 us (28%)
  other arithmetic  103 us (15%)
  waiting for transfers between devices  97.6 us (14%)
  matrix products  50.1 us (7%)
  blocking collectives  17.8 us (3%)
  starting transfers between devices  14.9 us (2%)
  between operations  13.7 us (2%)
    another operation x1, loops' own time, on_device(): lax.scan(sweep, (ratio_start, value_start), (diffusivity, right_side, glo...  102 us
    another operation x1, loops' own time, on_device(): lax.scan(compose, identity, (diffusivity, right_side, global_shells))  101 us
    dynamic_slice x224, local copies, waits for them, and re-layouts, on_device(): lax.scan(compose, identity, (diffusivity, right_side, global_shells))  79.9 us
    dynamic_update_slice x128, other arithmetic, on_device(): lax.scan(sweep, (ratio_start, value_start), (diffusivity, right_side, glo...  70.4 us
    all_to_all x1, waiting for transfers between devices, on_device(): lax.all_to_all(modes_grid, 'mode', split_axis=1, concat_axis=3, tiled=True)  47.4 us
    all_gather x1, waiting for transfers between devices, prefix_2(): pieces = jax.tree.map(lambda part: lax.all_gather(part, axis), value)  31.4 us
    unnamed x12, local copies, waits for them, and re-layouts  29.7 us
    all_to_all x2, local copies, waits for them, and re-layouts, on_device(): lax.all_to_all(flow_lat, 'mode', split_axis=3, concat_axis=1, tiled=True)  24.3 us
  transfers between devices with their start and end apart: 4, of which 4 were waited for; matrix products, arithmetic and copies ran while one was open for 8% of the time, Pallas kernels for 0%

commit v1 on v0

--- a/solution.py
+++ b/solution.py
@@ -66,7 +66,12 @@
         legendre,
         preferred_element_type=jnp.float32,
     ).astype(jnp.bfloat16)
-    field_piece = lax.all_to_all(field_lat, "mode", split_axis=3, concat_axis=1, tiled=True)
+    field_piece = jnp.concatenate(
+        lax.all_to_all(
+            jnp.stack(jnp.split(field_lat, lax.axis_size("mode"), axis=3)), "mode", 0, 0
+        ),
+        axis=1,
+    )
     flow_piece = lax.all_to_all(flow_lat, "mode", split_axis=3, concat_axis=1, tiled=True)
     field_grid = jnp.einsum(
         "rmct,mcp->rtp", field_piece, synth_table, preferred_element_type=jnp.float32

time: 707 us -> 698 us (0.987)
  local copies, waits for them, and re-layouts: 199 us -> 155 us
  waiting for transfers between devices: 97.6 us -> 123 us
    all_to_all x2 -> x0, local copies, waits for them, and re-layouts: 22.9 us -> none  [on_device(): lax.all_to_all(field_lat, 'mode', split_axis=3, concat_axis=1, tiled=True)]
    all_to_all x1, waiting for transfers between devices: 7.19 us -> 28.7 us  [on_device(): lax.all_to_all(flow_lat, 'mode', split_axis=3, concat_axis=1, tiled=True)]
    unnamed x12, local copies, waits for them, and re-layouts: 29.7 us -> 17.9 us
    convert_element_type x1 -> x0, local copies, waits for them, and re-layouts: 11.3 us -> none  [on_device(): field_lat = jnp.einsum('rmcj,mjt->rmct', scalar_field.astype(jnp.bfloat16...]
  transfers between devices with their start and end apart: 4 -> 4, of which waited for: 4 -> 4; matrix products, arithmetic and copies ran while one was open for 8% -> 6% of each run, Pallas kernels for 0% -> 0%
where the time goes in v1:
time: 698 us; the launch traced here: 692 us
  loops' own time  207 us (30%)
  local copies, waits for them, and re-layouts  155 us (22%)
  waiting for transfers between devices  123 us (18%)
  other arithmetic  109 us (16%)
  matrix products  51.7 us (7%)
  blocking collectives  17.8 us (3%)
  starting transfers between devices  14.1 us (2%)
  between operations  13.7 us (2%)
    another operation x1, loops' own time, on_device(): lax.scan(sweep, (ratio_start, value_start), (diffusivity, right_side, glo...  105 us
    another operation x1, loops' own time, on_device(): lax.scan(compose, identity, (diffusivity, right_side, global_shells))  101 us
    dynamic_slice x224, local copies, waits for them, and re-layouts, on_device(): lax.scan(compose, identity, (diffusivity, right_side, global_shells))  81.3 us
    dynamic_update_slice x128, other arithmetic, on_device(): lax.scan(sweep, (ratio_start, value_start), (diffusivity, right_side, glo...  75.1 us
    all_to_all x1, waiting for transfers between devices, on_device(): lax.all_to_all(modes_grid, 'mode', split_axis=1, concat_axis=3, tiled=True)  47.4 us
    all_gather x1, waiting for transfers between devices, prefix_2(): pieces = jax.tree.map(lambda part: lax.all_gather(part, axis), value)  31.4 us
    all_to_all x1, waiting for transfers between devices, on_device(): lax.all_to_all(flow_lat, 'mode', split_axis=3, concat_axis=1, tiled=True)  28.7 us
    all_to_all x2, local copies, waits for them, and re-layouts, on_device(): lax.all_to_all(flow_lat, 'mode', split_axis=3, concat_axis=1, tiled=True)  24.3 us
  transfers between devices with their start and end apart: 4, of which 4 were waited for; matrix products, arithmetic and copies ran while one was open for 6% of the time, Pallas kernels for 0%

profile of v1, /device:TPU:0, one launch (start us, length us, event | category | flops | bytes accessed | tf_op | source)
XLA Modules:
  0.0 691.5 jit_solution(11071039877651665291)
XLA Ops:
  6.5 2.0 convert_element_type.80
  8.5 5.2 fusion.39
  13.7 11.3 %copy.49 = bf16[32,16,2,768]{0,2,1,3:T(2,128)(2,1)} copy(bf16[32,16,2,768]{3,0,2,1:T(8,128)(2,1)S(1)} %fusion.39) | data formatting | bytes 3145728 | tf_op jit(solution)/shard_map/convert_element_type | solution.py:68
  25.0 8.3 %reshape.127 = bf16[4,2,98304]{2,1,0:T(2,128)(2,1)} reshape(bf16[768,16,2,32]{3,2,1,0:T(2,128)(2,1)} %bitcast.175) | data formatting | bytes 3145728
  33.3 6.5 all-to-all-start.1
  40.3 5.2 fusion.42
  46.1 1.9 pad_maximum_fusion.1
  48.0 28.7 %all-to-all-done.1 = bf16[4,2,98304]{2,1,0:T(2,128)(2,1)S(1)} async-done(((bf16[4,2,98304]{2,1,0:T(2,128)(2,1)}), bf16[4,2,98304]{2,1,0:T(2,128)(2,1)S(1)}, u32[]{:S(2)}, u32[]{:S(2)}) %all-to-all-start.1) | async-done | bytes 1572896 | tf_op jit(solution)/shard_map/all_to_all | solution.py:75
  77.9 3.8 all-to-all-start
  81.7 1.6 sine_negate_fusion
  83.3 6.4 reshape.128
  89.7 20.9 %copy.63 = bf16[32,16,2,4,192]{4,3,1,2,0:T(4,128)(2,1)} copy(bf16[32,16,2,4,192]{0,2,1,4,3:T(2,128)(2,1)} %bitcast.176) | data formatting | bytes 3145728 | tf_op jit(solution)/shard_map/all_to_all | solution.py:75
  110.6 3.4 copy.51
  113.9 15.3 %all-to-all-done = bf16[4,32,16,2,192]{4,1,3,2,0:T(8,128)(2,1)S(1)} async-done(((bf16[4,32,16,2,192]{4,1,3,2,0:T(8,128)(2,1)}), bf16[4,32,16,2,192]{4,1,3,2,0:T(8,128)(2,1)S(1)}, u32[]{:S(2)}, u32[]{:S(2)}) %all-to-all-start) | async-done | bytes 1572896 | tf_op jit(solution)/shard_map/all_to_all | solution.py:70
  129.2 16.4 %fusion.27 = f32[32,192,1536,1]{2,1,3,0:T(8,128)} fusion(bf16[32,64,2,192]{3,0,2,1:T(8,128)(2,1)S(1)} %bitcast.177, f32[64,1,1536]{2,0,1:T(8,128)S(1)} %get-tuple-element.648, f32[64,1,1536]{2,0,1:T(8,128)S(1)} %get-tuple-element.649), kind=kOutput, calls=%fused_computation.55 | convolution fusion | flops 2416508928 | bytes 40108032 | tf_op jit(solution)/shard_map/rmct,mcp->rtp/dot_general | solution.py:76
  145.7 17.3 %convert_bitcast_fusion = bf16[32,64,2,192]{3,1,0,2:T(8,128)(2,1)S(1)} fusion(f32[32,192,1536,1]{2,1,3,0:T(8,128)} %fusion.27, bf16[32,64,2,192]{3,1,2,0:T(8,128)(2,1)} %bitcast.181, f32[64,1,1536]{2,0,1:T(8,128)S(1)} %get-tuple-element.648, f32[64,1,1536]{2,0,1:T(8,128)S(1)} %get-tuple-element.649), kind=kOutput, calls=%fused_computation.57 | convolution fusion | flops 4852678656 | bytes 41680896 | tf_op jit(solution)/shard_map/rtp,mcp->rmct/dot_general | solution.py:83
  163.0 2.5 copy.52
  165.5 3.6 all-to-all-start.2
  169.5 47.4 %all-to-all-done.2 = bf16[32,64,2,192]{3,0,2,1:T(8,128)(2,1)S(1)} async-done(((bf16[32,64,2,192]{3,0,2,1:T(8,128)(2,1)}), bf16[32,64,2,192]{3,0,2,1:T(8,128)(2,1)S(1)}, u32[]{:S(2)}, u32[]{:S(2)}) %all-to-all-start.2) | async-done | bytes 1572896 | tf_op jit(solution)/shard_map/all_to_all | solution.py:86
  216.9 1.3 copy-done.1
  218.2 3.6 copy.82
  221.8 2.8 all_to_all.37
  224.6 7.6 %bitcast_add_fusion.1 = f32[32,16,2,384]{3,0,2,1:T(8,128)S(1)} fusion(f32[32,16,2,384]{3,2,1,0:T(2,128)} %param.14, bf16[32,16,2,768]{3,0,2,1:T(8,128)(2,1)} %all_to_all.37, bf16[16,384,768]{2,1,0:T(8,128)(2,1)} %param.16), kind=kOutput, calls=%fused_computation.60 | convolution fusion | flops 604372992 | bytes 14155776 | tf_op jit(solution)/shard_map/rmct,mjt->rmcj/dot_general | solution.py:87
  232.3 164.2 %while.77 = (s32[]{:T(128)}, f32[4,4,16,384]{3,2,1,0:T(8,128)S(1)}, s32[32]{0:T(128)S(1)}, f32[32]{0:T(128)S(1)}, f32[32,16,2,384]{3,0,2,1:T(8,128)S(1)}, /*inde...) while((s32[]{:T(128)}, f32[4,4,16,384]{3,2,1,0:T(8,128)S(1)}, ...), condition=%wide.region_2.3_spmd.clone, body=%wide.region_0.2_spmd.clone.sunk | while | flops 1161229 | bytes 2408801 | solution.py:125
  397.3 31.4 %all-gather.5.cloned.1.call-done = f32[32,4,16,384]{3,2,1,0:T(8,128)} async-done(((f32[4,4,16,384]{3,2,1,0:T(8,128)}), f32[32,4,16,384]{3,2,1,0:T(8,128)}) %all-gather.5.cloned.1.call-update) | async-done | bytes 3145744 | tf_op jit(solution)/shard_map/all_gather | solution.py:12
  428.8 9.0 %while.76 = (s32[]{:T(128)}, f32[4,4,16,384]{3,2,1,0:T(8,128)S(1)}, s32[]{:T(128)}, f32[8,4,4,16,384]{4,3,2,1,0:T(8,128)}, s32[]{:T(128)}) while((s32[]{:T(128)}, f32[4,4,16,384]{3,2,1,0:T(8,128)S(1)}, s32[]{:T(128)}, f32[8,4,4,16,384]{4,3,2,1,0:T(8,128)}, s32[]{:T(128)}) %tuple.175), condition=%wide.region_6.7_spmd, body=%wide.region_3.6_spmd.sunk | while | flops 1075203 | bytes 3588171 | solution.py:24
  438.2 1.9 broadcast.105.clone
  440.1 193.8 %while.78 = (s32[]{:T(128)}, f32[16,384]{1,0:T(8,128)S(1)}, f32[16,2,384]{2,1,0:T(2,128)S(1)}, f32[32,16,384]{2,1,0:T(8,128)S(1)}, f32[32,16,2,384]{3,2,1,0:T(2,...) while((s32[]{:T(128)}, f32[16,384]{1,0:T(8,128)S(1)}, ...), condition=%wide.region_8.9_spmd.clone, body=%wide.region_7.8_spmd.clone.sunk | while | flops 92172 | bytes 419129 | solution.py:140
  634.7 29.2 %while.79 = (s32[]{:T(128)}, f32[16,2,384]{2,1,0:T(2,128)S(1)}, f32[16,384]{1,0:T(8,128)S(1)}, f32[32,16,2,384]{3,2,1,0:T(2,128)S(1)}, f32[32,16,384]{2,1,0:T(8,...) while((s32[]{:T(128)}, f32[16,2,384]{2,1,0:T(2,128)S(1)}, ...), condition=%wide.region_10.11_spmd.clone, body=%wide.region_9.10_spmd.clone.sunk | while | flops 55300 | bytes 344196 | solution.py:153
  663.9 9.5 %all-gather.1 = f32[128,2,384]{2,1,0:T(2,128)S(1)} all-gather(f32[16,2,384]{2,1,0:T(2,128)S(1)} %get-tuple-element.408), channel_id=3, replica_groups=mesh['radial'=8,'mode'=4] {'radial'}, dimensions={0}, use_global_device_ids=true | all-gather | bytes 442368 | tf_op jit(solution)/shard_map/all_gather | solution.py:12
  673.5 8.3 %all-gather.2 = f32[128,384]{1,0:T(8,128)S(1)} all-gather(f32[16,384]{1,0:T(8,128)S(1)} %get-tuple-element.409), channel_id=4, replica_groups=mesh['radial'=8,'mode'=4] {'radial'}, dimensions={0}, use_global_device_ids=true | all-gather | bytes 221184 | tf_op jit(solution)/shard_map/all_gather | solution.py:12
  682.6 2.1 multiply_add_fusion.3
  (586 shorter events, 195.1 us)
Async XLA Ops:
  33.3 6.5 copy-start.2
  33.3 43.4 %all-to-all-start.1 = ((bf16[4,2,98304]{2,1,0:T(2,128)(2,1)}), bf16[4,2,98304]{2,1,0:T(2,128)(2,1)S(1)}, u32[]{:S(2)}, u32[]{:S(2)}) async-start(bf16[4,2,98304]{2,1,0:T(2,128)(2,1)} %reshape.127), calls=%async_computation.1 | async-start | bytes 3145728 | tf_op jit(solution)/shard_map/all_to_all | solution.py:75
  76.8 1.1 copy-start.3
  77.9 51.3 %all-to-all-start = ((bf16[4,32,16,2,192]{4,1,3,2,0:T(8,128)(2,1)}), bf16[4,32,16,2,192]{4,1,3,2,0:T(8,128)(2,1)S(1)}, u32[]{:S(2)}, u32[]{:S(2)}) async-start(bf16[4,32,16,2,192]{4,1,3,2,0:T(8,128)(2,1)} %pad_maximum_fusion.1), calls=%async_computation | async-start | bytes 4194304 | tf_op jit(solution)/shard_map/all_to_all | solution.py:70
  165.5 51.3 %all-to-all-start.2 = ((bf16[32,64,2,192]{3,0,2,1:T(8,128)(2,1)}), bf16[32,64,2,192]{3,0,2,1:T(8,128)(2,1)S(1)}, u32[]{:S(2)}, u32[]{:S(2)}) async-start(bf16[32,64,2,192]{3,0,2,1:T(8,128)(2,1)} %copy.52), calls=%async_computation.2 | async-start | bytes 4194304 | tf_op jit(solution)/shard_map/all_to_all | solution.py:86
  169.1 259.6 %all-gather.5.cloned.1.call-start = ((), (), s32[]{:S(2)}) async-start(), calls=%async_computation.3 | async-start | bytes 3538944 | tf_op jit(solution)/shard_map/all_gather | solution.py:12
  216.9 1.3 copy-start.1
  224.6 7.7 %copy-start.4 = (f32[32]{0:T(128)S(1)}, f32[32]{0:T(128)}, u32[]{:S(2)}) copy-start(f32[32]{0:T(128)} %param.17) | copy-start | bytes 388
  396.5 0.7 copy-start
Sparse Core Ops, SparseCore 0:
  397.4 31.2 all-gather.4
